TPU v7x, 1024 devices: a whole 8x8x8 slice. The times are simulated.
1024 devices in a mesh: load: 2 (over z_lo), sy: 64 (over y, x), sz: 8 (over z_hi, core).
Axes of the slice: x: 8, y: 8, z: 8 (z_hi: 4, z_lo: 2; z = z_hi * 2 + z_lo), core: 2. Of those that a mesh axis runs over, the one named last changes fastest.
Arguments:
- displacements: float32 [4, 3, 32, 1024, 512], P('load', None, 'sz', 'sy'), may hold values from -2.4 to 2.4
- density: float32 [32, 1024, 512], P('sz', 'sy'), may hold values from 0.05 to 1
- solid: int32 [32, 1024, 512], P('sz', 'sy'), may hold values 0 or 1
- fixed: int32 [32, 1024, 512], P('sz', 'sy'), may hold values 0 or 1
Outputs:
- sensitivity: float32 [32, 1024, 512], P('sz', 'sy')
All inputs are finite; a program needn't handle non-finite values. No bound on the sum of `solid` or of `fixed` on one device may be relied on, other than what follows from the above.
Results may differ from a plain program's by a relative error of at most 0.0001.
Values sent between devices are 32-bit elements; how exact they have to be, the bound alone decides.
A program may use at most 32 MiB of HBM per device.

v0:
```python
import jax
import jax.numpy as jnp
import numpy as np
from jax import lax
from jax.sharding import PartitionSpec as P

OFFSETS = [(0, 0, 0), (1, 0, 0), (1, 1, 0), (0, 1, 0), (0, 0, 1), (1, 0, 1), (1, 1, 1), (0, 1, 1)]


def shifted(value, axis, by):
    size = lax.axis_size(axis)
    pairs = [(i, i + by) for i in range(size) if 0 <= i + by < size]
    return lax.ppermute(value, axis, pairs)


def extended_2(cells, sides, width):
    for axis, dim in sides:
        count = lax.axis_size(axis)
        ends = count - 1
        head = lax.slice_in_dim(cells, 0, width, axis=dim)
        tail = lax.slice_in_dim(cells, cells.shape[dim] - width, cells.shape[dim], axis=dim)
        cells = jnp.concatenate(
            [
                lax.ppermute(tail, axis, [(i, (i + 1) % count) for i in range(ends)]),
                cells,
                lax.ppermute(head, axis, [((i + 1) % count, i) for i in range(ends)]),
            ],
            axis=dim,
        )
    return cells


def element_matrix():
    corners = np.array(
        [
            [-1.0, -1.0, -1.0],
            [1.0, -1.0, -1.0],
            [1.0, 1.0, -1.0],
            [-1.0, 1.0, -1.0],
            [-1.0, -1.0, 1.0],
            [1.0, -1.0, 1.0],
            [1.0, 1.0, 1.0],
            [-1.0, 1.0, 1.0],
        ]
    )
    poisson = 0.3
    lame = poisson / ((1.0 + poisson) * (1.0 - 2.0 * poisson))
    shear = 1.0 / (2.0 * (1.0 + poisson))
    elastic = np.zeros((6, 6))
    elastic[:3, :3] = lame
    for k in range(3):
        elastic[k, k] += 2.0 * shear
        elastic[3 + k, 3 + k] = shear
    gauss = 1.0 / np.sqrt(3.0)
    stiffness = np.zeros((24, 24))
    for gi in range(2):
        for gj in range(2):
            for gk in range(2):
                point = np.array([(2 * gi - 1) * gauss, (2 * gj - 1) * gauss, (2 * gk - 1) * gauss])
                strain = np.zeros((6, 24))
                for node in range(8):
                    grads = np.zeros(3)
                    for k in range(3):
                        value = corners[node, k] / 8.0
                        for m in range(3):
                            if m != k:
                                value = value * (1.0 + point[m] * corners[node, m])
                        grads[k] = 2.0 * value
                    col = 3 * node
                    strain[0, col] = grads[0]
                    strain[1, col + 1] = grads[1]
                    strain[2, col + 2] = grads[2]
                    strain[3, col] = grads[1]
                    strain[3, col + 1] = grads[0]
                    strain[4, col + 1] = grads[2]
                    strain[4, col + 2] = grads[1]
                    strain[5, col] = grads[2]
                    strain[5, col + 2] = grads[0]
                stiffness += strain.T @ elastic @ strain / 8.0
    return stiffness


def weight_line(coord, count):
    total = jnp.zeros(coord.shape, jnp.float32)
    for step in range(-3, 4):
        inside = (coord + step >= 0) & (coord + step < count)
        total = total + jnp.where(inside, 4.0 - abs(step), 0.0).astype(jnp.float32)
    return total


def spread_axis(padded, axis, length):
    total = None
    for k in range(7):
        piece = (4.0 - abs(k - 3)) * lax.slice_in_dim(padded, k, k + length, axis=axis)
        total = piece if total is None else total + piece
    return total


def body(displacements, density, solid, fixed):
    stiffness = jnp.asarray(element_matrix(), jnp.float32)
    load_dev, _, zlen, ylen, xlen = displacements.shape
    held = displacements * (1 - fixed).astype(jnp.float32)[None, None]
    upper_z = shifted(held[:, :, :1], "sz", -1)
    extended = jnp.concatenate([held, upper_z], axis=2)
    upper_y = shifted(extended[:, :, :, :1], "sy", -1)
    extended = jnp.concatenate([extended, upper_y], axis=3)
    extended = jnp.pad(extended, ((0, 0), (0, 0), (0, 0), (0, 0), (0, 1)))
    partial_energy = jnp.zeros((zlen, ylen, xlen), jnp.float32)
    for case in range(load_dev):
        nodes = [extended[case, :, c : c + zlen, b : b + ylen, a : a + xlen] for a, b, c in OFFSETS]
        local = jnp.stack(nodes, axis=0).reshape(24, zlen * ylen * xlen)
        image = jnp.dot(
            stiffness, local, precision=lax.Precision.HIGHEST, preferred_element_type=jnp.float32
        )
        partial_energy = partial_energy + jnp.sum(local * image, axis=0).reshape(zlen, ylen, xlen)
    total_z = zlen * lax.axis_size("sz")
    total_y = ylen * lax.axis_size("sy")
    hz = weight_line(lax.axis_index("sz") * zlen + jnp.arange(zlen, dtype=jnp.int32), total_z)
    hy = weight_line(lax.axis_index("sy") * ylen + jnp.arange(ylen, dtype=jnp.int32), total_y)
    energy = lax.psum(partial_energy, "load")
    hx = weight_line(jnp.arange(xlen, dtype=jnp.int32), xlen)
    term = solid.astype(jnp.float32) * (-3.0 * density * density) * energy
    quotient = term / (hz[:, None, None] * hy[None, :, None] * hx[None, None, :])
    padded_x = jnp.pad(quotient, ((0, 0), (0, 0), (3, 3)))
    filtered = spread_axis(padded_x, 2, xlen)
    padded = extended_2(filtered, (("sy", 1), ("sz", 0)), 3)
    filtered = spread_axis(padded, 1, ylen)
    filtered = spread_axis(filtered, 0, zlen)
    return filtered


def solution(mesh):
    return jax.shard_map(
        body,
        mesh=mesh,
        in_specs=(
            P("load", None, "sz", "sy", None),
            P("sz", "sy", None),
            P("sz", "sy", None),
            P("sz", "sy", None),
        ),
        out_specs=P("sz", "sy", None),
        check_vma=False,
    )
```

profile of v0, /device:TPU:63, one launch (start us, length us, event | category | flops | bytes accessed | tf_op | source)
XLA Modules:
  0.0 137.3 jit_solution(8142982491318294595)
XLA Ops:
  6.5 0.0 all-reduce.4.cloned.1.call-start
  6.5 0.9 subtract_convert_fusion
  7.5 1.2 broadcast_multiply_fusion
  8.7 2.6 %collective-permute-start = (f32[2,3,1,16,512]{4,3,2,1,0:T(8,128)S(1)}, f32[2,3,1,16,512]{4,3,2,1,0:T(8,128)S(1)}, u32[]{:S(2)}, u32[]{:S(2)}) collective-permute-start(f32[2,3,1,16,512]{4,3,2,1,0:T(8,128)S(1)} %slice.184), channel_id=1, source_target_pairs={{1,0},{2,1},{3,2},{4,3},{5,4},{6,5},{7,6},{9,8},{10,9},{11,10},{12... | collective-permute-start | bytes 589832 | tf_op jit(solution)/shard_map/ppermute | solution.py:13
  11.4 8.9 %collective-permute-done = f32[2,3,1,16,512]{4,3,2,1,0:T(8,128)S(1)} collective-permute-done((f32[2,3,1,16,512]{4,3,2,1,0:T(8,128)S(1)}, f32[2,3,1,16,512]{4,3,2,1,0:T(8,128)S(1)}, u32[]{:S(2)}, u32[]{:S(2)}) %collective-permute-start) | collective-permute-done | bytes 196640 | tf_op jit(solution)/shard_map/ppermute | solution.py:13
  20.3 3.1 %collective-permute-start.1 = (f32[2,3,5,1,512]{4,3,2,1,0:T(1,128)S(1)}, f32[2,3,5,1,512]{4,3,2,1,0:T(1,128)S(1)}, u32[]{:S(2)}, u32[]{:S(2)}) collective-permute-start(f32[2,3,5,1,512]{4,3,2,1,0:T(1,128)S(1)} %pad_maximum_fusion.4), channel_id=1, source_target_pairs={{8,0},{16,8},{24,16},{32,24},{40,32},{48,40},{56,48},{64,56},{72,6... | collective-permute-start | bytes 184328 | tf_op jit(solution)/shard_map/ppermute | solution.py:13
  23.4 5.2 %collective-permute-done.1 = f32[2,3,5,1,512]{4,3,2,1,0:T(1,128)S(1)} collective-permute-done((f32[2,3,5,1,512]{4,3,2,1,0:T(1,128)S(1)}, f32[2,3,5,1,512]{4,3,2,1,0:T(1,128)S(1)}, u32[]{:S(2)}, u32[]{:S(2)}) %collective-permute-start.1) | collective-permute-done | bytes 61472 | tf_op jit(solution)/shard_map/ppermute | solution.py:13
  28.6 0.2 pad_maximum_fusion
  28.8 0.2 fusion.6
  28.9 0.2 fusion.7
  29.2 0.8 fusion.10
  30.0 0.2 fusion.8
  30.2 1.0 fusion.9
  31.2 0.9 slice_dynamic-update-slice_fusion
  32.1 0.0 copy-start.1
  32.1 0.9 slice_dynamic-update-slice_fusion.4
  33.0 1.0 maximum_dynamic-update-slice_fusion
  34.0 0.9 fusion.4
  35.0 0.9 fusion.5
  35.9 0.0 copy-done.1
  35.9 0.8 slice_dynamic-update-slice_fusion.3
  36.7 2.9 %reshape.177 = f32[24,32768]{1,0:T(8,128)S(1)} reshape(f32[8,3,4,16,512]{4,3,2,1,0:T(8,128)} %slice_dynamic-update-slice_fusion.3) | data formatting | bytes 6291456 | tf_op jit(solution)/shard_map/reshape | solution.py:111
  39.6 0.0 copy-start.4
  39.6 4.6 %reshape.178 = f32[24,32768]{1,0:T(8,128)} reshape(f32[8,3,4,16,512]{4,3,2,1,0:T(8,128)} %copy-done.1) | data formatting | bytes 6291456 | tf_op jit(solution)/shard_map/reshape | solution.py:111
  44.2 0.0 copy-done.4
  44.2 0.0 copy-start
  44.2 0.0 copy-start.2
  44.2 0.0 copy-start.3
  44.2 3.0 %fusion = f32[32768]{0:T(1024)S(1)} fusion(f32[24,32768]{1,0:T(8,128)S(1)} %reshape.177, f32[24,24]{1,0:T(8,128)S(1)} %copy-done.4), kind=kOutput, calls=%fused_computation.10 | convolution fusion | flops 228032512 | bytes 3279104 | tf_op jit(solution)/shard_map/dot_general | solution.py:112
  47.2 0.0 copy-done
  47.2 3.1 %fusion.1 = f32[32768]{0:T(1024)S(1)} fusion(f32[24,32768]{1,0:T(8,128)S(1)} %copy-done, f32[24,24]{1,0:T(8,128)S(1)} %copy-done.4), kind=kOutput, calls=%fused_computation.11 | convolution fusion | flops 228032512 | bytes 3279104 | tf_op jit(solution)/shard_map/dot_general | solution.py:112
  50.4 0.7 add.357
  51.1 0.0 all-reduce.4.cloned.1.call-update
  51.1 0.1 broadcast_multiply_fusion.1
  51.2 48.8 %all-reduce.4.cloned.1.call-done = f32[4,16,512]{2,1,0:T(8,128)} async-done(((f32[4,16,512]{2,1,0:T(8,128)}), f32[4,16,512]{2,1,0:T(8,128)}) %all-reduce.4.cloned.1.call-update) | async-done | bytes 131088 | tf_op jit(solution)/shard_map/psum | solution.py:120
  100.0 0.0 copy-done.2
  100.0 0.0 copy-done.3
  100.0 1.0 fusion.18
  101.0 0.3 fusion.24
  101.3 4.3 %collective-permute-start.2 = (f32[4,3,512]{2,1,0:T(4,128)S(1)}, f32[4,3,512]{2,1,0:T(4,128)S(1)}, u32[]{:S(2)}, u32[]{:S(2)}) collective-permute-start(f32[4,3,512]{2,1,0:T(4,128)S(1)} %get-tuple-element.13), channel_id=1, source_target_pairs={{0,8},{8,16},{16,24},{24,32},{32,40},{40,48},{48,56},{56,64},{64,7... | collective-permute-start | bytes 73736 | tf_op jit(solution)/shard_map/ppermute | solution.py:24
  105.6 1.9 %collective-permute-start.3 = (f32[4,3,512]{2,1,0:T(4,128)S(1)}, f32[4,3,512]{2,1,0:T(4,128)S(1)}, u32[]{:S(2)}, u32[]{:S(2)}) collective-permute-start(f32[4,3,512]{2,1,0:T(4,128)S(1)} %get-tuple-element.14), channel_id=1, source_target_pairs={{8,0},{16,8},{24,16},{32,24},{40,32},{48,40},{56,48},{64,56},{72,6... | collective-permute-start | bytes 73736 | tf_op jit(solution)/shard_map/ppermute | solution.py:26
  107.5 0.0 collective-permute-done.2
  107.5 6.0 %collective-permute-done.3 = f32[4,3,512]{2,1,0:T(4,128)S(1)} collective-permute-done((f32[4,3,512]{2,1,0:T(4,128)S(1)}, f32[4,3,512]{2,1,0:T(4,128)S(1)}, u32[]{:S(2)}, u32[]{:S(2)}) %collective-permute-start.3) | collective-permute-done | bytes 24608 | tf_op jit(solution)/shard_map/ppermute | solution.py:26
  113.6 7.2 %collective-permute-start.4 = (f32[3,22,512]{2,1,0:T(8,128)S(1)}, f32[3,22,512]{2,1,0:T(8,128)S(1)}, u32[]{:S(2)}, u32[]{:S(2)}) collective-permute-start(f32[3,22,512]{2,1,0:T(8,128)S(1)} %get-tuple-element.11), channel_id=1, source_target_pairs={{0,1},{1,2},{2,3},{3,4},{4,5},{5,6},{6,7},{8,9},{9,10},{10,11},{11... | collective-permute-start | bytes 405512 | tf_op jit(solution)/shard_map/ppermute | solution.py:24
  120.8 1.9 %collective-permute-start.5 = (f32[3,22,512]{2,1,0:T(8,128)S(1)}, f32[3,22,512]{2,1,0:T(8,128)S(1)}, u32[]{:S(2)}, u32[]{:S(2)}) collective-permute-start(f32[3,22,512]{2,1,0:T(8,128)S(1)} %get-tuple-element.12), channel_id=1, source_target_pairs={{1,0},{2,1},{3,2},{4,3},{5,4},{6,5},{7,6},{9,8},{10,9},{11,10},{12... | collective-permute-start | bytes 405512 | tf_op jit(solution)/shard_map/ppermute | solution.py:26
  122.7 0.2 collective-permute-done.4
  122.9 6.5 %collective-permute-done.5 = f32[3,22,512]{2,1,0:T(8,128)S(1)} collective-permute-done((f32[3,22,512]{2,1,0:T(8,128)S(1)}, f32[3,22,512]{2,1,0:T(8,128)S(1)}, u32[]{:S(2)}, u32[]{:S(2)}) %collective-permute-start.5) | collective-permute-done | bytes 135200 | tf_op jit(solution)/shard_map/ppermute | solution.py:26
  129.4 0.1 pad_maximum_fusion.1
  129.5 0.2 slice_add_fusion
  129.7 0.7 slice_add_fusion.1
  (11 shorter events, 0.2 us)
Async XLA Ops:
  6.5 93.4 %all-reduce.4.cloned.1.call-start = ((), (), s32[]{:S(2)}) async-start(), calls=%async_computation | async-start | bytes 262144 | tf_op jit(solution)/shard_map/psum | solution.py:120
  8.7 11.5 %collective-permute-start = (f32[2,3,1,16,512]{4,3,2,1,0:T(8,128)S(1)}, f32[2,3,1,16,512]{4,3,2,1,0:T(8,128)S(1)}, u32[]{:S(2)}, u32[]{:S(2)}) collective-permute-start(f32[2,3,1,16,512]{4,3,2,1,0:T(8,128)S(1)} %slice.184), channel_id=1, source_target_pairs={{1,0},{2,1},{3,2},{4,3},{5,4},{6,5},{7,6},{9,8},{10,9},{11,10},{12... | collective-permute-start | bytes 589832 | tf_op jit(solution)/shard_map/ppermute | solution.py:13
  20.3 8.3 %collective-permute-start.1 = (f32[2,3,5,1,512]{4,3,2,1,0:T(1,128)S(1)}, f32[2,3,5,1,512]{4,3,2,1,0:T(1,128)S(1)}, u32[]{:S(2)}, u32[]{:S(2)}) collective-permute-start(f32[2,3,5,1,512]{4,3,2,1,0:T(1,128)S(1)} %pad_maximum_fusion.4), channel_id=1, source_target_pairs={{8,0},{16,8},{24,16},{32,24},{40,32},{48,40},{56,48},{64,56},{72,6... | collective-permute-start | bytes 184328 | tf_op jit(solution)/shard_map/ppermute | solution.py:13
  32.1 3.8 %copy-start.1 = (f32[8,3,4,16,512]{4,3,2,1,0:T(8,128)}, f32[8,3,4,16,512]{4,3,2,1,0:T(8,128)S(1)}, u32[]{:S(2)}) copy-start(f32[8,3,4,16,512]{4,3,2,1,0:T(8,128)S(1)} %get-tuple-element.5) | copy-start | bytes 9437188
  39.6 4.6 %copy-start.4 = (f32[24,24]{1,0:T(8,128)S(1)}, f32[24,24]{1,0:T(8,128)}, u32[]{:S(2)}) copy-start(f32[24,24]{1,0:T(8,128)} %constant.43.clone) | copy-start | bytes 6916
  44.2 3.0 %copy-start = (f32[24,32768]{1,0:T(8,128)S(1)}, f32[24,32768]{1,0:T(8,128)}, u32[]{:S(2)}) copy-start(f32[24,32768]{1,0:T(8,128)} %reshape.178) | copy-start | bytes 9437188
  44.2 55.7 %copy-start.2 = (f32[4,16,512]{2,1,0:T(8,128)S(1)}, f32[4,16,512]{2,1,0:T(8,128)}, u32[]{:S(2)}) copy-start(f32[4,16,512]{2,1,0:T(8,128)} %param.6) | copy-start | bytes 393220
  44.2 55.7 %copy-start.3 = (s32[4,16,512]{2,1,0:T(8,128)S(1)}, s32[4,16,512]{2,1,0:T(8,128)}, u32[]{:S(2)}) copy-start(s32[4,16,512]{2,1,0:T(8,128)} %param.7) | copy-start | bytes 393220
  101.3 6.2 %collective-permute-start.2 = (f32[4,3,512]{2,1,0:T(4,128)S(1)}, f32[4,3,512]{2,1,0:T(4,128)S(1)}, u32[]{:S(2)}, u32[]{:S(2)}) collective-permute-start(f32[4,3,512]{2,1,0:T(4,128)S(1)} %get-tuple-element.13), channel_id=1, source_target_pairs={{0,8},{8,16},{16,24},{24,32},{32,40},{40,48},{48,56},{56,64},{64,7... | collective-permute-start | bytes 73736 | tf_op jit(solution)/shard_map/ppermute | solution.py:24
  105.6 8.0 %collective-permute-start.3 = (f32[4,3,512]{2,1,0:T(4,128)S(1)}, f32[4,3,512]{2,1,0:T(4,128)S(1)}, u32[]{:S(2)}, u32[]{:S(2)}) collective-permute-start(f32[4,3,512]{2,1,0:T(4,128)S(1)} %get-tuple-element.14), channel_id=1, source_target_pairs={{8,0},{16,8},{24,16},{32,24},{40,32},{48,40},{56,48},{64,56},{72,6... | collective-permute-start | bytes 73736 | tf_op jit(solution)/shard_map/ppermute | solution.py:26
  113.6 9.3 %collective-permute-start.4 = (f32[3,22,512]{2,1,0:T(8,128)S(1)}, f32[3,22,512]{2,1,0:T(8,128)S(1)}, u32[]{:S(2)}, u32[]{:S(2)}) collective-permute-start(f32[3,22,512]{2,1,0:T(8,128)S(1)} %get-tuple-element.11), channel_id=1, source_target_pairs={{0,1},{1,2},{2,3},{3,4},{4,5},{5,6},{6,7},{8,9},{9,10},{10,11},{11... | collective-permute-start | bytes 405512 | tf_op jit(solution)/shard_map/ppermute | solution.py:24
  120.8 8.6 %collective-permute-start.5 = (f32[3,22,512]{2,1,0:T(8,128)S(1)}, f32[3,22,512]{2,1,0:T(8,128)S(1)}, u32[]{:S(2)}, u32[]{:S(2)}) collective-permute-start(f32[3,22,512]{2,1,0:T(8,128)S(1)} %get-tuple-element.12), channel_id=1, source_target_pairs={{1,0},{2,1},{3,2},{4,3},{5,4},{6,5},{7,6},{9,8},{10,9},{11,10},{12... | collective-permute-start | bytes 405512 | tf_op jit(solution)/shard_map/ppermute | solution.py:26
Sparse Core Ops, SparseCore 0:
  51.2 48.7 all-reduce.3
where the time goes:
time: 138 us; the launch traced here: 137 us
  waiting for transfers between devices  75.6 us (55%)
  starting transfers between devices  21 us (15%)
  local copies, waits for them, and re-layouts  14.3 us (10%)
  between operations  13.6 us (10%)
  other arithmetic  6.67 us (5%)
  matrix products  6.09 us (4%)
    psum x1, waiting for transfers between devices, body(): energy = lax.psum(partial_energy, 'load')  48.8 us
    ppermute x2, waiting for transfers between devices, shifted(): return lax.ppermute(value, axis, pairs)  14.1 us
    ppermute x2, waiting for transfers between devices, extended_2(): lax.ppermute(head, axis, [((i + 1) % count, i) for i in range(ends)])  12.5 us
    ppermute x2, starting transfers between devices, extended_2(): lax.ppermute(tail, axis, [(i, (i + 1) % count) for i in range(ends)])  11.5 us
    reshape x2, local copies, waits for them, and re-layouts, body(): local = jnp.stack(nodes, axis=0).reshape(24, zlen * ylen * xlen)  7.51 us
    dot_general x2, matrix products, body(): jnp.dot(stiffness, local, precision=lax.Precision.HIGHEST, preferred_elem...  6.09 us
    ppermute x2, starting transfers between devices, shifted(): return lax.ppermute(value, axis, pairs)  5.65 us
    unnamed x19, local copies, waits for them, and re-layouts  4.34 us
  transfers between devices with their start and end apart: 7, of which 6 were waited for; matrix products, arithmetic and copies ran while one was open for 0% of the time, Pallas kernels for 0%

commit v1 on v0

v1 whole, which is shorter than its diff:
```python
import functools

import jax
import jax.numpy as jnp
from jax import lax
from jax.experimental import pallas as pl
from jax.experimental.pallas import tpu as pltpu
from jax.sharding import PartitionSpec as P

MESH = pl.DeviceIdType.MESH
F32 = jnp.float32
LAME = 0.3 / (1.3 * 0.4)
SHEAR = 1.0 / 2.6
CHUNK = 128


def line_weight(coord, count):
    total = None
    for step in range(-3, 4):
        inside = (coord + step >= 0) & (coord + step < count)
        piece = jnp.where(inside, F32(4.0 - abs(step)), F32(0.0))
        total = piece if total is None else total + piece
    return total


def box_twice(value, axis):
    size = value.shape[axis]
    value = value + pltpu.roll(value, size - 1, axis)
    value = value + pltpu.roll(value, size - 2, axis)
    value = value + pltpu.roll(value, 1, axis)
    return value + pltpu.roll(value, 2, axis)


def filter_x(value):
    rows, cols = value.shape
    padded = jnp.concatenate([value, jnp.zeros((rows, 128), F32)], axis=1)
    return box_twice(padded, 1)[:, :cols]


def filter_z(layers):
    pairs = [layers[k] + layers[k + 1] for k in range(9)]
    runs = [pairs[k] + pairs[k + 2] for k in range(7)]
    pairs = [runs[k] + runs[k + 1] for k in range(6)]
    return [pairs[k] + pairs[k + 2] for k in range(4)]


def mode_energy(low, high):
    x, y, z = range(3)
    mode = []
    for k in range(3):
        (ls, lx, ly, lxy), (hs, hx, hy, hxy) = low[k], high[k]
        mode.append(
            dict(
                z=hs - ls, x=hx + lx, y=hy + ly, xy=hxy + lxy,
                xz=hx - lx, yz=hy - ly, xyz=hxy - lxy,
            )
        )
    sq = lambda v: v * v
    a, b, c = mode
    div = sq(a["x"] + b["y"] + c["z"])
    normal = sq(a["x"]) + sq(b["y"]) + sq(c["z"])
    shear = sq(a["y"] + b["x"]) + sq(b["z"] + c["y"]) + sq(a["z"] + c["x"])
    bend = sq(b["xy"] + c["xz"]) + sq(a["xy"] + c["yz"]) + sq(a["xz"] + b["yz"])
    six = (
        sq(a["xy"]) + sq(a["xz"]) + sq(b["xy"]) + sq(b["yz"]) + sq(c["xz"]) + sq(c["yz"])
    )
    twist = sq(a["yz"] + b["xz"]) + sq(a["yz"] + c["xy"]) + sq(b["xz"] + c["xy"])
    last = sq(a["xyz"]) + sq(b["xyz"]) + sq(c["xyz"])
    return div, normal, shear, bend, six, twist, last


def weigh(groups):
    div, normal, shear, bend, six, twist, last = groups
    s = 1.0 / 16.0
    return (
        F32(s * LAME) * div
        + F32(s * 2.0 * SHEAR) * normal
        + F32(s * SHEAR) * (shear + six)
        + F32(s * LAME / 3.0) * bend
        + F32(s * SHEAR / 3.0) * twist
        + F32(s * (LAME + 4.0 * SHEAR) / 9.0) * last
    )


def kernel(
    disp, dens, solid, fixed, out,
    raw, den, sol, fix, held, faces, energy, coef, part, other, ext,
    load_sem, send, recv, ready,
):
    nsz, nsy, nload = lax.axis_size("sz"), lax.axis_size("sy"), lax.axis_size("load")
    sz, sy, ld = lax.axis_index("sz"), lax.axis_index("sy"), lax.axis_index("load")
    up, down = lax.rem(sz + 1, nsz), lax.rem(sz + nsz - 1, nsz)
    right, left = lax.rem(sy + 1, nsy), lax.rem(sy + nsy - 1, nsy)
    mate = lax.rem(ld + 1, nload)

    loads = [
        pltpu.make_async_copy(s, d, load_sem.at[k])
        for k, (s, d) in enumerate(((disp, raw), (fixed, fix), (dens, den), (solid, sol)))
    ]
    for copy in loads:
        copy.start()
    barrier = pltpu.get_barrier_semaphore()
    around = ({"sz": up}, {"sz": down}, {"sy": right}, {"sy": left}, {"load": mate})
    for device in around:
        pl.semaphore_signal(barrier, inc=1, device_id=device, device_id_type=MESH)

    ext[:, 19:21, :] = jnp.zeros((10, 2, 512), F32)
    loads[0].wait()
    loads[1].wait()

    def hold(z, carry):
        free = F32(1.0) - fix[z].astype(F32)
        for case in range(2):
            for k in range(3):
                held[3 * case + k, z, 0:16, :] = raw[case, k, z] * free
        return carry

    lax.fori_loop(0, 4, hold, 0)
    pl.semaphore_wait(barrier, 5)

    started = []

    def send_to(k, src, dst, device):
        copy = pltpu.make_async_remote_copy(
            src_ref=src, dst_ref=dst, send_sem=send.at[k], recv_sem=recv.at[k],
            device_id=device, device_id_type=MESH,
        )
        copy.start()
        started.append(copy)
        return copy

    node_y = send_to(0, held.at[:, 0:4, 0:1], held.at[:, 0:4, 16:17], {"sy": left})
    node_z = send_to(1, held.at[:, 0, 0:16], held.at[:, 4, 0:16], {"sz": down})
    for device in around[:2]:
        pl.semaphore_signal(ready, inc=1, device_id=device, device_id_type=MESH)

    loads[2].wait()
    loads[3].wait()
    row = lax.broadcasted_iota(jnp.int32, (16, 512), 0)
    lane = lax.broadcasted_iota(jnp.int32, (16, 512), 1)
    area = line_weight(lane, 512) * line_weight(row + sy * 16, nsy * 16)
    for z in range(4):
        weight = area * line_weight(sz * 4 + z, nsz * 4)
        d = den[z]
        coef[z] = sol[z].astype(F32) * (F32(-3.0) * d * d) / weight

    last_lane = lax.broadcasted_iota(jnp.int32, (8, 512), 1) == 511

    def next_x(value):
        return jnp.where(last_lane, F32(0.0), pltpu.roll(value, 511, 1))

    def make_faces(half, z):
        r = 8 * half
        for k in range(6):
            near = held[k, z, r : r + 8, :]
            far = held[k, z, r + 1 : r + 9, :]
            total, diff = near + far, far - near
            total_x, diff_x = next_x(total), next_x(diff)
            faces[half, z, 4 * k] = total_x + total
            faces[half, z, 4 * k + 1] = total_x - total
            faces[half, z, 4 * k + 2] = diff_x + diff
            faces[half, z, 4 * k + 3] = diff_x - diff

    def faces_loop(half, first, last):
        def step(z, carry):
            make_faces(half, z)
            return carry

        lax.fori_loop(first, last, step, 0)

    def energy_loop(half, first, last):
        def step(i, carry):
            z, j = first + i // 4, i % 4
            cols = pl.ds(pl.multiple_of(j * CHUNK, CHUNK), CHUNK)
            groups = None
            for case in range(2):
                sides = [
                    [
                        [faces[half, zz, 12 * case + 4 * k + m, :, cols] for m in range(4)]
                        for k in range(3)
                    ]
                    for zz in (z, z + 1)
                ]
                got = mode_energy(*sides)
                groups = got if groups is None else [p + q for p, q in zip(groups, got)]
            energy[z, 8 * half : 8 * half + 8, cols] = weigh(groups)
            return carry

        lax.fori_loop(0, 4 * (last - first), step, 0)

    def finish_layer(z):
        part[z] = filter_x(energy[z] * coef[z])

    faces_loop(0, 0, 4)
    energy_loop(0, 0, 3)
    node_y.wait_recv()

    @pl.when(sy == nsy - 1)
    def _():
        held[:, 0:4, 16:17, :] = jnp.zeros((6, 4, 1, 512), F32)

    node_c = send_to(2, held.at[:, 0, 16:17], held.at[:, 4, 16:17], {"sz": down})
    faces_loop(1, 0, 4)
    energy_loop(1, 0, 3)
    for z in range(3):
        finish_layer(z)
    pair_a = send_to(3, part.at[0:3], other.at[0:3], {"load": mate})
    node_z.wait_recv()

    @pl.when(sz == nsz - 1)
    def _():
        held[:, 4, 0:16, :] = jnp.zeros((6, 16, 512), F32)

    faces_loop(0, 4, 5)
    energy_loop(0, 3, 4)
    node_c.wait_recv()

    @pl.when((sy == nsy - 1) | (sz == nsz - 1))
    def _():
        held[:, 4, 16:17, :] = jnp.zeros((6, 1, 512), F32)

    faces_loop(1, 4, 5)
    energy_loop(1, 3, 4)
    finish_layer(3)
    pair_b = send_to(4, part.at[3:4], other.at[3:4], {"load": mate})

    pl.semaphore_wait(ready, 2)
    pair_a.wait_recv()
    for z in range(3):
        ext[3 + z, 0:16, :] = part[z] + other[z]
    halo = [
        send_to(5, ext.at[3:6, 0:16], ext.at[7:10, 0:16], {"sz": down}),
        send_to(6, ext.at[3:6, 0:3], ext.at[7:10, 16:19], {"sz": down, "sy": left}),
        send_to(7, ext.at[3:6, 13:16], ext.at[7:10, 21:24], {"sz": down, "sy": right}),
    ]
    pair_b.wait_recv()
    ext[6, 0:16, :] = part[3] + other[3]
    halo += [
        send_to(8, ext.at[4:7, 0:16], ext.at[0:3, 0:16], {"sz": up}),
        send_to(9, ext.at[4:7, 0:3], ext.at[0:3, 16:19], {"sz": up, "sy": left}),
        send_to(10, ext.at[4:7, 13:16], ext.at[0:3, 21:24], {"sz": up, "sy": right}),
        send_to(11, ext.at[3:7, 0:3], ext.at[3:7, 16:19], {"sy": left}),
        send_to(12, ext.at[3:7, 13:16], ext.at[3:7, 21:24], {"sy": right}),
    ]
    for copy in halo:
        copy.wait_recv()

    @pl.when(sz == nsz - 1)
    def _():
        ext[7:10] = jnp.zeros((3, 24, 512), F32)

    @pl.when(sz == 0)
    def _():
        ext[0:3] = jnp.zeros((3, 24, 512), F32)

    @pl.when(sy == nsy - 1)
    def _():
        ext[:, 16:19, :] = jnp.zeros((10, 3, 512), F32)

    @pl.when(sy == 0)
    def _():
        ext[:, 21:24, :] = jnp.zeros((10, 3, 512), F32)

    for j in range(4):
        cols = slice(j * CHUNK, (j + 1) * CHUNK)
        layers = filter_z([ext[k, :, cols] for k in range(10)])
        for z in range(4):
            out[z, :, cols] = box_twice(layers[z], 0)[0:16]
    for copy in started:
        copy.wait_send()


def body(displacements, density, solid, fixed):
    dma = pltpu.SemaphoreType.DMA
    return pl.pallas_call(
        kernel,
        out_shape=jax.ShapeDtypeStruct((4, 16, 512), F32),
        in_specs=[pl.BlockSpec(memory_space=pl.ANY)] * 4,
        out_specs=pl.BlockSpec(memory_space=pltpu.VMEM),
        scratch_shapes=[
            pltpu.VMEM((2, 3, 4, 16, 512), F32),
            pltpu.VMEM((4, 16, 512), F32),
            pltpu.VMEM((4, 16, 512), jnp.int32),
            pltpu.VMEM((4, 16, 512), jnp.int32),
            pltpu.VMEM((6, 5, 24, 512), F32),
            pltpu.VMEM((2, 5, 24, 8, 512), F32),
            pltpu.VMEM((4, 16, 512), F32),
            pltpu.VMEM((4, 16, 512), F32),
            pltpu.VMEM((4, 16, 512), F32),
            pltpu.VMEM((4, 16, 512), F32),
            pltpu.VMEM((10, 24, 512), F32),
            dma((4,)),
            dma((13,)),
            dma((13,)),
            pltpu.SemaphoreType.REGULAR,
        ],
        compiler_params=pltpu.CompilerParams(collective_id=0, has_side_effects=True),
    )(displacements, density, solid, fixed)


def solution(mesh):
    return jax.shard_map(
        body,
        mesh=mesh,
        in_specs=(
            P("load", None, "sz", "sy", None),
            P("sz", "sy", None),
            P("sz", "sy", None),
            P("sz", "sy", None),
        ),
        out_specs=P("sz", "sy", None),
        check_vma=False,
    )
```

time: 138 us -> 36 us (0.26)
  the two profiles are of different devices: /device:TPU:63 before, /device:TPU:64 now
where the time goes in v1:
time: 36 us; the launch traced here: 35.8 us
  Pallas kernels  34.2 us (95%)
  local copies, waits for them, and re-layouts  1.57 us (4%)
    pallas_call x1, Pallas kernels, body(): pl.pallas_call(kernel, out_shape=jax.ShapeDtypeStruct((4, 16, 512), F32),...  34.2 us
    unnamed x1, local copies, waits for them, and re-layouts  1.57 us

profile of v1, /device:TPU:64, one launch (start us, length us, event | category | flops | bytes accessed | tf_op | source)
XLA Modules:
  0.0 35.8 jit_solution(12106435411477480367)
XLA Ops:
  0.0 34.2 %shard_map.46 = f32[4,16,512]{2,1,0:T(8,128)} custom-call(f32[2,3,4,16,512]{4,3,2,1,0:T(8,128)} %disp.1, f32[4,16,512]{2,1,0:T(8,128)} %dens.1, s32[4,16,512]{2,1,0:T(8,128)} %solid.1, s32[4,16,512]{2,1,0:T(8,128)} %fixed.1), custom_call_target="tpu_custom_call" | custom-call | tf_op jit(solution)/shard_map/pallas_call | solution.py:275
  34.2 1.6 %copy.6 = f32[4,16,512]{2,1,0:T(8,128)} copy(f32[4,16,512]{2,1,0:T(8,128)} %shard_map.46) | data formatting | bytes 262144

commit v2 on v1

--- a/solution.py
+++ b/solution.py
@@ -89,9 +89,9 @@
 ):
     nsz, nsy, nload = lax.axis_size("sz"), lax.axis_size("sy"), lax.axis_size("load")
     sz, sy, ld = lax.axis_index("sz"), lax.axis_index("sy"), lax.axis_index("load")
-    up, down = lax.rem(sz + 1, nsz), lax.rem(sz + nsz - 1, nsz)
-    right, left = lax.rem(sy + 1, nsy), lax.rem(sy + nsy - 1, nsy)
-    mate = lax.rem(ld + 1, nload)
+    has_up, has_down, has_right, has_left = sz < nsz - 1, sz > 0, sy < nsy - 1, sy > 0
+    up, down, right, left = {"sz": sz + 1}, {"sz": sz - 1}, {"sy": sy + 1}, {"sy": sy - 1}
+    mate = {"load": lax.rem(ld + 1, nload)}
 
     loads = [
         pltpu.make_async_copy(s, d, load_sem.at[k])
@@ -100,11 +100,37 @@
     for copy in loads:
         copy.start()
     barrier = pltpu.get_barrier_semaphore()
-    around = ({"sz": up}, {"sz": down}, {"sy": right}, {"sy": left}, {"load": mate})
-    for device in around:
-        pl.semaphore_signal(barrier, inc=1, device_id=device, device_id_type=MESH)
+
+    def greet(sem, device, when=None):
+        if when is None:
+            pl.semaphore_signal(sem, inc=1, device_id=device, device_id_type=MESH)
+        else:
+            pl.when(when)(lambda: greet(sem, device))
+
+    greet(barrier, mate)
+    greet(barrier, right, has_right)
+    greet(barrier, up, has_up)
 
     ext[:, 19:21, :] = jnp.zeros((10, 2, 512), F32)
+
+    @pl.when(jnp.logical_not(has_up))
+    def _():
+        ext[7:10] = jnp.zeros((3, 24, 512), F32)
+        held[:, 4] = jnp.zeros((6, 24, 512), F32)
+
+    @pl.when(jnp.logical_not(has_down))
+    def _():
+        ext[0:3] = jnp.zeros((3, 24, 512), F32)
+
+    @pl.when(jnp.logical_not(has_right))
+    def _():
+        ext[:, 16:19, :] = jnp.zeros((10, 3, 512), F32)
+        held[:, :, 16:17, :] = jnp.zeros((6, 5, 1, 512), F32)
+
+    @pl.when(jnp.logical_not(has_left))
+    def _():
+        ext[:, 21:24, :] = jnp.zeros((10, 3, 512), F32)
+
     loads[0].wait()
     loads[1].wait()
 
@@ -116,23 +142,28 @@
         return carry
 
     lax.fori_loop(0, 4, hold, 0)
-    pl.semaphore_wait(barrier, 5)
+    pl.semaphore_wait(barrier, 1 + has_down.astype(jnp.int32) + has_left.astype(jnp.int32))
 
     started = []
 
-    def send_to(k, src, dst, device):
+    def send_to(k, src, dst, device, sends=None, takes=None):
         copy = pltpu.make_async_remote_copy(
             src_ref=src, dst_ref=dst, send_sem=send.at[k], recv_sem=recv.at[k],
             device_id=device, device_id_type=MESH,
         )
-        copy.start()
-        started.append(copy)
-        return copy
-
-    node_y = send_to(0, held.at[:, 0:4, 0:1], held.at[:, 0:4, 16:17], {"sy": left})
-    node_z = send_to(1, held.at[:, 0, 0:16], held.at[:, 4, 0:16], {"sz": down})
-    for device in around[:2]:
-        pl.semaphore_signal(ready, inc=1, device_id=device, device_id_type=MESH)
+
+        def each(act, when):
+            if when is None:
+                act()
+            else:
+                pl.when(when)(act)
+
+        each(copy.start, sends)
+        started.append(lambda: each(copy.wait_send, sends))
+        return lambda: each(copy.wait_recv, takes)
+
+    node_z = send_to(1, held.at[:, 0, 0:16], held.at[:, 4, 0:16], down, has_down, has_up)
+    node_y = send_to(0, held.at[:, 0:4, 0:1], held.at[:, 0:4, 16:17], left, has_left, has_right)
 
     loads[2].wait()
     loads[3].wait()
@@ -193,81 +224,54 @@
 
     faces_loop(0, 0, 4)
     energy_loop(0, 0, 3)
-    node_y.wait_recv()
-
-    @pl.when(sy == nsy - 1)
-    def _():
-        held[:, 0:4, 16:17, :] = jnp.zeros((6, 4, 1, 512), F32)
-
-    node_c = send_to(2, held.at[:, 0, 16:17], held.at[:, 4, 16:17], {"sz": down})
+    node_y()
+    greet(ready, right, has_right)
+    node_c = send_to(
+        2, held.at[:, 0, 16:17], held.at[:, 4, 16:17], down, has_down & has_right, has_up & has_right
+    )
     faces_loop(1, 0, 4)
     energy_loop(1, 0, 3)
     for z in range(3):
         finish_layer(z)
-    pair_a = send_to(3, part.at[0:3], other.at[0:3], {"load": mate})
-    node_z.wait_recv()
-
-    @pl.when(sz == nsz - 1)
-    def _():
-        held[:, 4, 0:16, :] = jnp.zeros((6, 16, 512), F32)
-
+    pair_a = send_to(3, part.at[0:3], other.at[0:3], mate)
+    node_z()
     faces_loop(0, 4, 5)
     energy_loop(0, 3, 4)
-    node_c.wait_recv()
-
-    @pl.when((sy == nsy - 1) | (sz == nsz - 1))
-    def _():
-        held[:, 4, 16:17, :] = jnp.zeros((6, 1, 512), F32)
-
+    node_c()
     faces_loop(1, 4, 5)
     energy_loop(1, 3, 4)
     finish_layer(3)
-    pair_b = send_to(4, part.at[3:4], other.at[3:4], {"load": mate})
-
-    pl.semaphore_wait(ready, 2)
-    pair_a.wait_recv()
+    pair_b = send_to(4, part.at[3:4], other.at[3:4], mate)
+
+    @pl.when(has_left)
+    def _():
+        pl.semaphore_wait(ready, 1)
+
+    pair_a()
     for z in range(3):
         ext[3 + z, 0:16, :] = part[z] + other[z]
-    halo = [
-        send_to(5, ext.at[3:6, 0:16], ext.at[7:10, 0:16], {"sz": down}),
-        send_to(6, ext.at[3:6, 0:3], ext.at[7:10, 16:19], {"sz": down, "sy": left}),
-        send_to(7, ext.at[3:6, 13:16], ext.at[7:10, 21:24], {"sz": down, "sy": right}),
-    ]
-    pair_b.wait_recv()
+    halo = [send_to(5, ext.at[3:6, 0:16], ext.at[7:10, 0:16], down, has_down, has_up)]
+    pair_b()
     ext[6, 0:16, :] = part[3] + other[3]
     halo += [
-        send_to(8, ext.at[4:7, 0:16], ext.at[0:3, 0:16], {"sz": up}),
-        send_to(9, ext.at[4:7, 0:3], ext.at[0:3, 16:19], {"sz": up, "sy": left}),
-        send_to(10, ext.at[4:7, 13:16], ext.at[0:3, 21:24], {"sz": up, "sy": right}),
-        send_to(11, ext.at[3:7, 0:3], ext.at[3:7, 16:19], {"sy": left}),
-        send_to(12, ext.at[3:7, 13:16], ext.at[3:7, 21:24], {"sy": right}),
+        send_to(6, ext.at[4:7, 0:16], ext.at[0:3, 0:16], up, has_up, has_down),
+        send_to(7, ext.at[4:7, 13:16], ext.at[0:3, 21:24], up | right, has_up & has_right, has_down & has_left),
+        send_to(8, ext.at[4:7, 0:3], ext.at[0:3, 16:19], up | left, has_up & has_left, has_down & has_right),
+        send_to(9, ext.at[3:6, 13:16], ext.at[7:10, 21:24], down | right, has_down & has_right, has_up & has_left),
+        send_to(10, ext.at[3:6, 0:3], ext.at[7:10, 16:19], down | left, has_down & has_left, has_up & has_right),
+        send_to(11, ext.at[3:7, 13:16], ext.at[3:7, 21:24], right, has_right, has_left),
+        send_to(12, ext.at[3:7, 0:3], ext.at[3:7, 16:19], left, has_left, has_right),
     ]
-    for copy in halo:
-        copy.wait_recv()
-
-    @pl.when(sz == nsz - 1)
-    def _():
-        ext[7:10] = jnp.zeros((3, 24, 512), F32)
-
-    @pl.when(sz == 0)
-    def _():
-        ext[0:3] = jnp.zeros((3, 24, 512), F32)
-
-    @pl.when(sy == nsy - 1)
-    def _():
-        ext[:, 16:19, :] = jnp.zeros((10, 3, 512), F32)
-
-    @pl.when(sy == 0)
-    def _():
-        ext[:, 21:24, :] = jnp.zeros((10, 3, 512), F32)
+    for arrived in halo:
+        arrived()
 
     for j in range(4):
         cols = slice(j * CHUNK, (j + 1) * CHUNK)
         layers = filter_z([ext[k, :, cols] for k in range(10)])
         for z in range(4):
             out[z, :, cols] = box_twice(layers[z], 0)[0:16]
-    for copy in started:
-        copy.wait_send()
+    for drained in started:
+        drained()
 
 
 def body(displacements, density, solid, fixed):

time: 36 us -> 30 us (0.83)
  the two profiles are of different devices: /device:TPU:64 before, /device:TPU:65 now
where the time goes in v2:
time: 30 us; the launch traced here: 29.9 us
  Pallas kernels  28.3 us (94%)
  local copies, waits for them, and re-layouts  1.57 us (5%)
    pallas_call x1, Pallas kernels, body(): pl.pallas_call(kernel, out_shape=jax.ShapeDtypeStruct((4, 16, 512), F32),...  28.3 us
    unnamed x1, local copies, waits for them, and re-layouts  1.57 us

profile of v2, /device:TPU:65, one launch (start us, length us, event | category | flops | bytes accessed | tf_op | source)
XLA Modules:
  0.0 29.9 jit_solution(12749784013139957500)
XLA Ops:
  0.0 28.3 %shard_map.46 = f32[4,16,512]{2,1,0:T(8,128)} custom-call(f32[2,3,4,16,512]{4,3,2,1,0:T(8,128)} %disp.1, f32[4,16,512]{2,1,0:T(8,128)} %dens.1, s32[4,16,512]{2,1,0:T(8,128)} %solid.1, s32[4,16,512]{2,1,0:T(8,128)} %fixed.1), custom_call_target="tpu_custom_call" | custom-call | tf_op jit(solution)/shard_map/pallas_call | solution.py:279
  28.3 1.6 %copy.6 = f32[4,16,512]{2,1,0:T(8,128)} copy(f32[4,16,512]{2,1,0:T(8,128)} %shard_map.46) | data formatting | bytes 262144

commit v3 on v2

--- a/solution.py
+++ b/solution.py
@@ -84,7 +84,7 @@
 
 def kernel(
     disp, dens, solid, fixed, out,
-    raw, den, sol, fix, held, faces, energy, coef, part, other, ext,
+    raw, fix, den, sol, faces, energy, coef, mine, theirs, slab,
     load_sem, send, recv, ready,
 ):
     nsz, nsy, nload = lax.axis_size("sz"), lax.axis_size("sy"), lax.axis_size("load")
@@ -92,10 +92,17 @@
     has_up, has_down, has_right, has_left = sz < nsz - 1, sz > 0, sy < nsy - 1, sy > 0
     up, down, right, left = {"sz": sz + 1}, {"sz": sz - 1}, {"sy": sy + 1}, {"sy": sy - 1}
     mate = {"load": lax.rem(ld + 1, nload)}
+    low, high = ld == 0, ld == 1
+    odd = lax.rem(sz, 2) == 1
+    even = jnp.logical_not(odd)
 
     loads = [
-        pltpu.make_async_copy(s, d, load_sem.at[k])
-        for k, (s, d) in enumerate(((disp, raw), (fixed, fix), (dens, den), (solid, sol)))
+        pltpu.make_async_copy(src, dst, load_sem.at[k])
+        for k, (src, dst) in enumerate(
+            [(fixed, fix.at[0:4, 0:16])]
+            + [(disp.at[:, :, z], raw.at[:, :, z, 0:16]) for z in range(4)]
+            + [(dens, den), (solid, sol)]
+        )
     ]
     for copy in loads:
         copy.start()
@@ -110,39 +117,7 @@
     greet(barrier, mate)
     greet(barrier, right, has_right)
     greet(barrier, up, has_up)
-
-    ext[:, 19:21, :] = jnp.zeros((10, 2, 512), F32)
-
-    @pl.when(jnp.logical_not(has_up))
-    def _():
-        ext[7:10] = jnp.zeros((3, 24, 512), F32)
-        held[:, 4] = jnp.zeros((6, 24, 512), F32)
-
-    @pl.when(jnp.logical_not(has_down))
-    def _():
-        ext[0:3] = jnp.zeros((3, 24, 512), F32)
-
-    @pl.when(jnp.logical_not(has_right))
-    def _():
-        ext[:, 16:19, :] = jnp.zeros((10, 3, 512), F32)
-        held[:, :, 16:17, :] = jnp.zeros((6, 5, 1, 512), F32)
-
-    @pl.when(jnp.logical_not(has_left))
-    def _():
-        ext[:, 21:24, :] = jnp.zeros((10, 3, 512), F32)
-
-    loads[0].wait()
-    loads[1].wait()
-
-    def hold(z, carry):
-        free = F32(1.0) - fix[z].astype(F32)
-        for case in range(2):
-            for k in range(3):
-                held[3 * case + k, z, 0:16, :] = raw[case, k, z] * free
-        return carry
-
-    lax.fori_loop(0, 4, hold, 0)
-    pl.semaphore_wait(barrier, 1 + has_down.astype(jnp.int32) + has_left.astype(jnp.int32))
+    greet(barrier, up | right, has_up & has_right)
 
     started = []
 
@@ -162,19 +137,57 @@
         started.append(lambda: each(copy.wait_send, sends))
         return lambda: each(copy.wait_recv, takes)
 
-    node_z = send_to(1, held.at[:, 0, 0:16], held.at[:, 4, 0:16], down, has_down, has_up)
-    node_y = send_to(0, held.at[:, 0:4, 0:1], held.at[:, 0:4, 16:17], left, has_left, has_right)
-
-    loads[2].wait()
-    loads[3].wait()
+    loads[0].wait()
+    loads[1].wait()
+    free = F32(1.0) - fix[0, 0:16, :].astype(F32)
+    for case in range(2):
+        for k in range(3):
+            raw[case, k, 0, 0:16, :] = raw[case, k, 0, 0:16, :] * free
+
+    fix[4] = jnp.zeros((24, 512), jnp.int32)
+    one = lambda flag: flag.astype(jnp.int32)
+    pl.semaphore_wait(barrier, 1 + one(has_down) + one(has_left) + one(has_down & has_left))
+    node_z = [
+        send_to(0, raw.at[:, :, 0, 0:16], raw.at[:, :, 4, 0:16], down, has_down, has_up),
+    ]
+    node_c = [
+        send_to(
+            1, raw.at[:, :, 0, 0:1], raw.at[:, :, 4, 16:17], down | left,
+            has_down & has_left, has_up & has_right,
+        )
+    ]
+    node_y = [
+        send_to(2, disp.at[:, :, :, 0:1], raw.at[:, :, 0:4, 16:17], left, has_left, has_right),
+        send_to(3, fixed.at[:, 0:1], fix.at[0:4, 16:17], left, has_left, has_right),
+    ]
+
+    mine[:, 19:21, :] = jnp.zeros((4, 2, 512), F32)
+    theirs[:, 19:21, :] = jnp.zeros((4, 2, 512), F32)
+
+    @pl.when(jnp.logical_not(has_up))
+    def _():
+        slab[7:10] = jnp.zeros((3, 16, 512), F32)
+        raw[:, :, 4] = jnp.zeros((2, 3, 24, 512), F32)
+
+    @pl.when(jnp.logical_not(has_down))
+    def _():
+        slab[0:3] = jnp.zeros((3, 16, 512), F32)
+
+    @pl.when(jnp.logical_not(has_right))
+    def _():
+        mine[:, 16:19, :] = jnp.zeros((4, 3, 512), F32)
+        theirs[:, 16:19, :] = jnp.zeros((4, 3, 512), F32)
+        raw[:, :, :, 16:17, :] = jnp.zeros((2, 3, 5, 1, 512), F32)
+        fix[0:4, 16:17, :] = jnp.zeros((4, 1, 512), jnp.int32)
+
+    @pl.when(jnp.logical_not(has_left))
+    def _():
+        mine[:, 21:24, :] = jnp.zeros((4, 3, 512), F32)
+        theirs[:, 21:24, :] = jnp.zeros((4, 3, 512), F32)
+
     row = lax.broadcasted_iota(jnp.int32, (16, 512), 0)
     lane = lax.broadcasted_iota(jnp.int32, (16, 512), 1)
     area = line_weight(lane, 512) * line_weight(row + sy * 16, nsy * 16)
-    for z in range(4):
-        weight = area * line_weight(sz * 4 + z, nsz * 4)
-        d = den[z]
-        coef[z] = sol[z].astype(F32) * (F32(-3.0) * d * d) / weight
-
     last_lane = lax.broadcasted_iota(jnp.int32, (8, 512), 1) == 511
 
     def next_x(value):
@@ -182,15 +195,19 @@
 
     def make_faces(half, z):
         r = 8 * half
-        for k in range(6):
-            near = held[k, z, r : r + 8, :]
-            far = held[k, z, r + 1 : r + 9, :]
-            total, diff = near + far, far - near
-            total_x, diff_x = next_x(total), next_x(diff)
-            faces[half, z, 4 * k] = total_x + total
-            faces[half, z, 4 * k + 1] = total_x - total
-            faces[half, z, 4 * k + 2] = diff_x + diff
-            faces[half, z, 4 * k + 3] = diff_x - diff
+        free_near = F32(1.0) - fix[z, r : r + 8, :].astype(F32)
+        free_far = F32(1.0) - fix[z, r + 1 : r + 9, :].astype(F32)
+        for case in range(2):
+            for k in range(3):
+                near = raw[case, k, z, r : r + 8, :] * free_near
+                far = raw[case, k, z, r + 1 : r + 9, :] * free_far
+                total, diff = near + far, far - near
+                total_x, diff_x = next_x(total), next_x(diff)
+                m = 12 * case + 4 * k
+                faces[half, z, m] = total_x + total
+                faces[half, z, m + 1] = total_x - total
+                faces[half, z, m + 2] = diff_x + diff
+                faces[half, z, m + 3] = diff_x - diff
 
     def faces_loop(half, first, last):
         def step(z, carry):
@@ -219,57 +236,72 @@
 
         lax.fori_loop(0, 4 * (last - first), step, 0)
 
-    def finish_layer(z):
-        part[z] = filter_x(energy[z] * coef[z])
-
-    faces_loop(0, 0, 4)
+    def finish_layers(first, last):
+        for z in range(first, last):
+            mine[z, 0:16, :] = filter_x(energy[z] * coef[z])
+
+    def exchange(k, first, last):
+        whole = send_to(k, mine.at[first:last, 0:16], theirs.at[first:last, 0:16], mate)
+        if k == 6:
+            pl.semaphore_wait(ready, 1)
+        return [
+            whole,
+            send_to(k + 1, mine.at[first:last, 13:16], theirs.at[first:last, 21:24], mate | right, has_right, has_left),
+            send_to(k + 2, mine.at[first:last, 0:3], theirs.at[first:last, 16:19], mate | left, has_left, has_right),
+            send_to(k + 3, mine.at[first:last, 13:16], mine.at[first:last, 21:24], right, has_right, has_left),
+            send_to(k + 4, mine.at[first:last, 0:3], mine.at[first:last, 16:19], left, has_left, has_right),
+        ]
+
+    def take(arrivals):
+        for arrived in arrivals:
+            arrived()
+
+    def filter_y(first, last):
+        for z in range(first, last):
+            slab[3 + z] = box_twice(mine[z] + theirs[z], 0)[0:16]
+
+    make_faces(0, 0)
+    for z in range(1, 4):
+        loads[1 + z].wait()
+        make_faces(0, z)
     energy_loop(0, 0, 3)
-    node_y()
-    greet(ready, right, has_right)
-    node_c = send_to(
-        2, held.at[:, 0, 16:17], held.at[:, 4, 16:17], down, has_down & has_right, has_up & has_right
-    )
+    take(node_y)
+    greet(ready, mate)
     faces_loop(1, 0, 4)
     energy_loop(1, 0, 3)
-    for z in range(3):
-        finish_layer(z)
-    pair_a = send_to(3, part.at[0:3], other.at[0:3], mate)
-    node_z()
+    loads[5].wait()
+    loads[6].wait()
+    for z in range(4):
+        weight = area * line_weight(sz * 4 + z, nsz * 4)
+        d = den[z]
+        coef[z] = sol[z].astype(F32) * (F32(-3.0) * d * d) / weight
+    finish_layers(0, 3)
+    most = exchange(6, 0, 3)
+    take(node_z)
     faces_loop(0, 4, 5)
     energy_loop(0, 3, 4)
-    node_c()
+    take(node_c)
     faces_loop(1, 4, 5)
     energy_loop(1, 3, 4)
-    finish_layer(3)
-    pair_b = send_to(4, part.at[3:4], other.at[3:4], mate)
-
-    @pl.when(has_left)
-    def _():
-        pl.semaphore_wait(ready, 1)
-
-    pair_a()
-    for z in range(3):
-        ext[3 + z, 0:16, :] = part[z] + other[z]
-    halo = [send_to(5, ext.at[3:6, 0:16], ext.at[7:10, 0:16], down, has_down, has_up)]
-    pair_b()
-    ext[6, 0:16, :] = part[3] + other[3]
+    finish_layers(3, 4)
+    rest = exchange(11, 3, 4)
+    take(most)
+    filter_y(0, 3)
+    halo = [
+        send_to(16, slab.at[3:6], slab.at[7:10], down, has_down, has_up),
+    ]
+    take(rest)
+    filter_y(3, 4)
     halo += [
-        send_to(6, ext.at[4:7, 0:16], ext.at[0:3, 0:16], up, has_up, has_down),
-        send_to(7, ext.at[4:7, 13:16], ext.at[0:3, 21:24], up | right, has_up & has_right, has_down & has_left),
-        send_to(8, ext.at[4:7, 0:3], ext.at[0:3, 16:19], up | left, has_up & has_left, has_down & has_right),
-        send_to(9, ext.at[3:6, 13:16], ext.at[7:10, 21:24], down | right, has_down & has_right, has_up & has_left),
-        send_to(10, ext.at[3:6, 0:3], ext.at[7:10, 16:19], down | left, has_down & has_left, has_up & has_right),
-        send_to(11, ext.at[3:7, 13:16], ext.at[3:7, 21:24], right, has_right, has_left),
-        send_to(12, ext.at[3:7, 0:3], ext.at[3:7, 16:19], left, has_left, has_right),
-    ]
-    for arrived in halo:
-        arrived()
-
+        send_to(17, slab.at[4:7], slab.at[0:3], up | mate, high & odd & has_up, low & even & has_down),
+        send_to(5, slab.at[4:7], slab.at[0:3], up, (high | even) & has_up, (high | odd) & has_down),
+    ]
+    take(halo)
     for j in range(4):
         cols = slice(j * CHUNK, (j + 1) * CHUNK)
-        layers = filter_z([ext[k, :, cols] for k in range(10)])
+        layers = filter_z([slab[k, :, cols] for k in range(10)])
         for z in range(4):
-            out[z, :, cols] = box_twice(layers[z], 0)[0:16]
+            out[z, :, cols] = layers[z]
     for drained in started:
         drained()
 
@@ -278,24 +310,23 @@
     dma = pltpu.SemaphoreType.DMA
     return pl.pallas_call(
         kernel,
-        out_shape=jax.ShapeDtypeStruct((4, 16, 512), F32),
+        out_shape=pltpu.VMEM((4, 16, 512), F32),
         in_specs=[pl.BlockSpec(memory_space=pl.ANY)] * 4,
         out_specs=pl.BlockSpec(memory_space=pltpu.VMEM),
         scratch_shapes=[
-            pltpu.VMEM((2, 3, 4, 16, 512), F32),
+            pltpu.VMEM((2, 3, 5, 24, 512), F32),
+            pltpu.VMEM((5, 24, 512), jnp.int32),
             pltpu.VMEM((4, 16, 512), F32),
             pltpu.VMEM((4, 16, 512), jnp.int32),
-            pltpu.VMEM((4, 16, 512), jnp.int32),
-            pltpu.VMEM((6, 5, 24, 512), F32),
             pltpu.VMEM((2, 5, 24, 8, 512), F32),
             pltpu.VMEM((4, 16, 512), F32),
             pltpu.VMEM((4, 16, 512), F32),
-            pltpu.VMEM((4, 16, 512), F32),
-            pltpu.VMEM((4, 16, 512), F32),
-            pltpu.VMEM((10, 24, 512), F32),
-            dma((4,)),
-            dma((13,)),
-            dma((13,)),
+            pltpu.VMEM((4, 24, 512), F32),
+            pltpu.VMEM((4, 24, 512), F32),
+            pltpu.VMEM((10, 16, 512), F32),
+            dma((7,)),
+            dma((18,)),
+            dma((18,)),
             pltpu.SemaphoreType.REGULAR,
         ],
         compiler_params=pltpu.CompilerParams(collective_id=0, has_side_effects=True),

time: 30 us -> 28.5 us (0.950)
  the two profiles are of different devices: /device:TPU:65 before, /device:TPU:321 now
where the time goes in v3:
time: 28.5 us; the launch traced here: 28.3 us
  Pallas kernels  27.7 us (97%)
  local copies, waits for them, and re-layouts  0.66 us (2%)
    pallas_call x1, Pallas kernels, body(): pl.pallas_call(kernel, out_shape=pltpu.VMEM((4, 16, 512), F32), in_specs=...  27.7 us
    unnamed x1, local copies, waits for them, and re-layouts  0.66 us

profile of v3, /device:TPU:321, one launch (start us, length us, event | category | flops | bytes accessed | tf_op | source)
XLA Modules:
  0.0 28.3 jit_solution(8878125110076694451)
XLA Ops:
  0.0 27.7 %shard_map.46 = f32[4,16,512]{2,1,0:T(8,128)S(1)} custom-call(f32[2,3,4,16,512]{4,3,2,1,0:T(8,128)} %disp.1, f32[4,16,512]{2,1,0:T(8,128)} %dens.1, s32[4,16,512]{2,1,0:T(8,128)} %solid.1, s32[4,16,512]{2,1,0:T(8,128)} %fixed.1), custom_call_target="tpu_custom_call" | custom-call | tf_op jit(solution)/shard_map/pallas_call | solution.py:311
  27.7 0.7 %copy.6 = f32[4,16,512]{2,1,0:T(8,128)} copy(f32[4,16,512]{2,1,0:T(8,128)S(1)} %shard_map.46) | data formatting | bytes 262144

commit v4 on v3

--- a/solution.py
+++ b/solution.py
@@ -161,6 +161,8 @@
         send_to(3, fixed.at[:, 0:1], fix.at[0:4, 16:17], left, has_left, has_right),
     ]
 
+    greet(ready, mate)
+
     mine[:, 19:21, :] = jnp.zeros((4, 2, 512), F32)
     theirs[:, 19:21, :] = jnp.zeros((4, 2, 512), F32)
 
@@ -266,7 +268,6 @@
         make_faces(0, z)
     energy_loop(0, 0, 3)
     take(node_y)
-    greet(ready, mate)
     faces_loop(1, 0, 4)
     energy_loop(1, 0, 3)
     loads[5].wait()

time: 28.5 us -> 28.5 us (level)
  no operation moved by 1% of the time
where the time goes in v4:
time: 28.5 us; the launch traced here: 28.3 us
  Pallas kernels  27.7 us (97%)
  local copies, waits for them, and re-layouts  0.66 us (2%)
    pallas_call x1, Pallas kernels, body(): pl.pallas_call(kernel, out_shape=pltpu.VMEM((4, 16, 512), F32), in_specs=...  27.7 us
    unnamed x1, local copies, waits for them, and re-layouts  0.66 us

profile of v4, /device:TPU:321, one launch (start us, length us, event | category | flops | bytes accessed | tf_op | source)
XLA Modules:
  0.0 28.3 jit_solution(11605861195707176946)
XLA Ops:
  0.0 27.7 %shard_map.46 = f32[4,16,512]{2,1,0:T(8,128)S(1)} custom-call(f32[2,3,4,16,512]{4,3,2,1,0:T(8,128)} %disp.1, f32[4,16,512]{2,1,0:T(8,128)} %dens.1, s32[4,16,512]{2,1,0:T(8,128)} %solid.1, s32[4,16,512]{2,1,0:T(8,128)} %fixed.1), custom_call_target="tpu_custom_call" | custom-call | tf_op jit(solution)/shard_map/pallas_call | solution.py:312
  27.7 0.7 %copy.6 = f32[4,16,512]{2,1,0:T(8,128)} copy(f32[4,16,512]{2,1,0:T(8,128)S(1)} %shard_map.46) | data formatting | bytes 262144
